TPU v7x, 256 devices: a whole 4x4x8 slice. The times are simulated.
256 devices in a mesh: sub: 2 (over core), row: 16 (over x, y), col: 8 (over z).
Axes of the slice: x: 4, y: 4, z: 8, core: 2. Of those that a mesh axis runs over, the one named last changes fastest.
Arguments:
- front: float32 [16384, 16384], P(('sub', 'row'), 'col'), as said below
- child_blocks: float32 [2, 8192, 8192], P('sub', 'row', 'col'), may hold values from -1 to 1
- child_map: int32 [2, 8192], replicated, may hold values from 0 to 16383, as said below
Outputs:
- factored: float32 [16384, 16384], P(('sub', 'row'), 'col')
Inputs may be any that keep to these rules, and one draw needn't show every extreme that they name: Each row of child_map is strictly increasing. Call block b the parent indices b * 32 to b * 32 + 31. Of the entries at positions k * 1024 to (k + 1) * 1024 - 1 of a row, exactly 128 lie in blocks whose number modulo 8 is d, for every k and d. Of the entries at positions k * 512 to (k + 1) * 512 - 1, at most 24 lie in blocks whose number modulo 32 is p, for every k and p; for each child some p takes exactly 24 from every k. The front's diagonal dominates the rows of the pivot block by construction.
All inputs are finite; a program needn't handle non-finite values.
Results may differ from a plain program's by a relative error of at most 0.00012.
Values sent between devices are 32-bit elements; how exact they have to be, the bound alone decides.
A program may use at most 128 MiB of HBM per device.

v0:
```python
import jax
import jax.numpy as jnp
from jax import lax
from jax.sharding import PartitionSpec as P

PW = 512
NB = 32


def from_root(value, axis, source):
    kept = jnp.where(lax.axis_index(axis) == source, value, 0).astype(value.dtype)
    return lax.psum(kept, axis)


def natural_index(local, group, groups):
    return (local // NB * groups + group) * NB + local % NB


def local_index(natural, groups):
    return natural // NB // groups * NB + natural % NB


def slot_ranks(owner, groups):
    member = (owner[:, None] == jnp.arange(groups, dtype=jnp.int32)[None, :]).astype(jnp.int32)
    return jnp.sum(jnp.cumsum(member, axis=0) * member, axis=1) - 1


def body(front, child_blocks, child_map):
    n_sub = lax.axis_size("sub")
    n_row = lax.axis_size("row")
    n_col = lax.axis_size("col")
    row_groups = n_sub * n_row
    row_group = lax.axis_index("sub") * n_row + lax.axis_index("row")
    col_group = lax.axis_index("col")
    local_rows, local_cols = front.shape
    natural_rows = natural_index(jnp.arange(local_rows, dtype=jnp.int32), row_group, row_groups)
    natural_cols = natural_index(jnp.arange(local_cols, dtype=jnp.int32), col_group, n_col)
    lower = natural_rows[:, None] >= natural_cols[None, :]
    assembled = jnp.where(lower, front, jnp.float32(0.0))
    contribution = child_blocks[0]
    child_rows, child_cols = contribution.shape
    own_map = lax.dynamic_index_in_dim(child_map, lax.axis_index("sub"), 0, keepdims=False)
    row_start = lax.axis_index("row") * child_rows
    col_start = col_group * child_cols
    child_row_ids = row_start + jnp.arange(child_rows, dtype=jnp.int32)
    child_col_ids = col_start + jnp.arange(child_cols, dtype=jnp.int32)
    contribution = jnp.where(
        child_row_ids[:, None] >= child_col_ids[None, :], contribution, jnp.float32(0.0)
    )
    row_targets = lax.dynamic_slice_in_dim(own_map, row_start, child_rows)
    col_targets = lax.dynamic_slice_in_dim(own_map, col_start, child_cols)
    per_dest = child_cols // n_col
    col_owner = col_targets // NB % n_col
    col_slots = col_owner * per_dest + slot_ranks(col_owner, n_col)
    col_order = (
        jnp.zeros((child_cols,), jnp.int32)
        .at[col_slots]
        .set(jnp.arange(child_cols, dtype=jnp.int32))
    )
    spans = 2 * child_rows // NB // row_groups
    capacity = NB // 2 * spans + NB // 4 * max(0, 2 - spans)
    buffer_rows = row_groups * capacity
    row_owner = row_targets // NB % row_groups
    row_slots = row_owner * capacity + slot_ranks(row_owner, row_groups)
    source_rows = (
        jnp.full((buffer_rows,), child_rows, jnp.int32)
        .at[row_slots]
        .set(jnp.arange(child_rows, dtype=jnp.int32))
    )
    filled = source_rows < child_rows
    source_rows = jnp.minimum(source_rows, child_rows - 1)
    by_column = contribution[:, col_order]
    moved = lax.all_to_all(by_column, "col", split_axis=1, concat_axis=1, tiled=True)
    packed = jnp.where(filled[:, None], moved[source_rows], jnp.float32(0.0))
    received = lax.all_to_all(packed, ("sub", "row"), split_axis=0, concat_axis=0, tiled=True)
    slots_child = n_row * capacity
    received_cols = received.shape[1]
    received = received.reshape(n_sub, slots_child, received_cols)
    for child in range(n_sub):
        full_map = child_map[child]
        col_mask = full_map // NB % n_col == col_group
        taken = jnp.nonzero(col_mask, size=received_cols)[0]
        col_index = local_index(full_map[taken], n_col)
        match = (
            (full_map // NB % row_groups == row_group).astype(jnp.int32).reshape(n_row, child_rows)
        )
        ranks = jnp.cumsum(match, axis=1) - 1
        slots = jnp.arange(n_row, dtype=jnp.int32)[:, None] * capacity + ranks
        slots = jnp.where(match > 0, slots, slots_child).reshape(-1)
        row_index = (
            jnp.full((slots_child,), local_rows, jnp.int32)
            .at[slots]
            .set(local_index(full_map, row_groups), mode="drop")
        )
        slot_of_row = (
            jnp.full((local_rows,), slots_child, jnp.int32)
            .at[row_index]
            .set(jnp.arange(slots_child, dtype=jnp.int32), mode="drop")
        )
        col_source = (
            jnp.full((local_cols,), received_cols, jnp.int32)
            .at[col_index]
            .set(jnp.arange(received_cols, dtype=jnp.int32), mode="drop")
        )
        row_inside = slot_of_row < slots_child
        col_inside = col_source < received_cols
        placed = received[child][jnp.minimum(slot_of_row, slots_child - 1)][
            :, jnp.minimum(col_source, received_cols - 1)
        ]
        assembled = assembled + jnp.where(
            row_inside[:, None] & col_inside[None, :], placed, jnp.float32(0.0)
        )
    panel_local = PW // n_col
    gathered = lax.all_gather(assembled[:, :panel_local], "col", axis=1, tiled=True)
    panel = (
        gathered.reshape(local_rows, n_col, panel_local // NB, NB)
        .transpose(0, 2, 1, 3)
        .reshape(local_rows, PW)
    )
    head_blocks = max(1, PW // (row_groups * NB))
    heading = lax.all_gather(panel[: head_blocks * NB], ("sub", "row"), axis=0, tiled=True)
    corner = (
        heading.reshape(row_groups, head_blocks, NB, PW).transpose(1, 0, 2, 3).reshape(-1, PW)[:PW]
    )
    pivot = jnp.tril(corner) + jnp.tril(corner, -1).T
    factor = jnp.linalg.cholesky(pivot)
    solved = lax.linalg.triangular_solve(
        factor, panel, left_side=False, lower=True, transpose_a=True
    )
    factor_rows = jnp.where(
        natural_rows[:, None] < PW, factor[jnp.clip(natural_rows, 0, PW - 1)], solved
    )
    spread = row_groups // n_col
    pieces = [
        from_root(factor_rows, ("sub", "row"), col_group + step * n_col) for step in range(spread)
    ]
    stacked = jnp.stack([piece.reshape(local_rows // NB, NB, PW) for piece in pieces], axis=1)
    factor_cols = stacked.reshape(local_cols, PW)
    product = lax.dot_general(
        factor_rows,
        factor_cols,
        (((1,), (1,)), ((), ())),
        precision=lax.Precision.HIGHEST,
        preferred_element_type=jnp.float32,
    )
    update = assembled - product
    update = update.at[:, :panel_local].set(factor_rows[:, natural_cols[:panel_local]])
    return jnp.where(lower, update, jnp.float32(0.0))


def solution(mesh):
    return jax.shard_map(
        body,
        mesh=mesh,
        in_specs=(P(("sub", "row"), "col"), P("sub", "row", "col"), P()),
        out_specs=P(("sub", "row"), "col"),
        check_vma=False,
    )
```

profile of v0, /device:TPU:6, one launch (start us, length us, event | category | flops | bytes accessed | tf_op | source)
XLA Modules:
  0.0 718.6 jit_solution(14528451676120354646)
XLA Ops:
  11.0 4.3 scatter_custom_fusion.5
  20.1 4.9 gather_fusion.1
  25.0 8.6 %all-to-all-start = ((f32[512,8,128]{0,2,1:T(8,128)}), f32[512,8,128]{0,2,1:T(8,128)S(1)}, u32[]{:S(2)}, u32[]{:S(2)}) async-start(f32[512,8,128]{0,2,1:T(8,128)} %bitcast.218), calls=%async_computation | async-start | bytes 4194304 | tf_op jit(solution)/shard_map/all_to_all | solution.py:73
  39.4 56.9 %scatter_custom_fusion.2 = s32[1024]{0:T(1024)S(1)} fusion(s32[8192]{0:T(1024)S(1)} %bitcast.238, s32[8192]{0:T(1024)S(1)} %ne.666, s32[]{:T(128)} %constant.510.clone.1), kind=kCustom, calls=%fused_computation.418 | custom fusion | flops 8192 | bytes 4100 | tf_op jit(solution)/shard_map/scatter-add | solution.py:82
  101.6 6.2 gather_fusion
  107.7 56.8 %scatter_custom_fusion.8 = s32[1024]{0:T(1024)S(1)} fusion(s32[8192]{0:T(1024)S(1)} %bitcast.237, s32[8192]{0:T(1024)S(1)} %ne.666, s32[]{:T(128)} %constant.510.clone.1), kind=kCustom, calls=%fused_computation.416 | custom fusion | flops 8192 | bytes 4100 | tf_op jit(solution)/shard_map/scatter-add | solution.py:82
  165.9 6.2 gather_fusion.5
  172.6 30.6 %scatter_custom_fusion = s32[384]{0:T(512)S(1)} fusion(s32[8192]{0:T(1024)S(1)} %bitcast.236, s32[8192]{0:T(1024)S(1)} %get-tuple-element.71, s32[]{:T(128)} %constant.522.clone.1), kind=kCustom, calls=%fused_computation.433 | custom fusion | bytes 1540 | tf_op jit(solution)/shard_map/scatter | solution.py:93
  210.2 3.8 broadcast_select_fusion
  214.0 7.6 %all-to-all-start.1 = ((f32[32,24,1024]{2,1,0:T(8,128)}), f32[32,24,1024]{2,1,0:T(8,128)}, u32[]{:S(2)}, u32[]{:S(2)}) async-start(f32[32,24,1024]{2,1,0:T(8,128)} %broadcast_select_fusion), calls=%async_computation.1 | async-start | bytes 6291456 | tf_op jit(solution)/shard_map/all_to_all | solution.py:75
  221.8 4.3 scatter_custom_fusion.3
  226.1 30.4 %scatter_custom_fusion.6 = s32[384]{0:T(512)S(1)} fusion(s32[8192]{0:T(1024)S(1)} %bitcast.235, s32[8192]{0:T(1024)S(1)} %get-tuple-element.68, s32[]{:T(128)} %constant.522.clone.1), kind=kCustom, calls=%fused_computation.431 | custom fusion | bytes 1540 | tf_op jit(solution)/shard_map/scatter | solution.py:93
  262.5 4.3 scatter_custom_fusion.9
  274.9 8.9 %gather_fusion.4 = f32[2048,512]{1,0:T(8,128)} fusion(f32[512,1024]{0,1:T(8,128)S(1)} %copy.59, s32[2048]{0:T(1024)S(1)} %fusion.85), kind=kCustom, calls=%fused_computation.4 | custom fusion | bytes 8396800 | tf_op jit(solution)/shard_map/gather | solution.py:107
  283.8 5.5 copy.60
  293.9 8.9 %gather_fusion.7 = f32[2048,512]{1,0:T(8,128)} fusion(f32[512,1024]{0,1:T(8,128)S(1)} %copy.66, s32[2048]{0:T(1024)S(1)} %fusion.86), kind=kCustom, calls=%fused_computation.7 | custom fusion | bytes 8396800 | tf_op jit(solution)/shard_map/gather | solution.py:107
  302.8 5.4 copy.67
  308.2 5.6 fusion.1
  316.7 40.4 %all-gather.3.cloned.1.call-done = f32[512,512]{0,1:T(8,128)} async-done(((f32[512,64]{0,1:T(8,128)}), f32[512,512]{0,1:T(8,128)}) %all-gather.3.cloned.1.call-update) | async-done | bytes 1048592 | tf_op jit(solution)/shard_map/all_gather | solution.py:114
  362.9 43.7 %all-gather.5.cloned.1.call-done = f32[1024,512]{1,0:T(8,128)} async-done(((f32[32,512]{1,0:T(8,128)}), f32[1024,512]{1,0:T(8,128)}) %all-gather.5.cloned.1.call-update) | async-done | bytes 2097168 | tf_op jit(solution)/shard_map/all_gather | solution.py:121
  411.2 11.7 %cholesky.103 = f32[128,128]{1,0:T(8,128)S(1)} custom-call(f32[128,128]{1,0:T(8,128)S(1)} %cholesky.263), custom_call_target="Cholesky" | custom-call | tf_op jit(solution)/shard_map/jit(cholesky)/cholesky | solution.py:126
  423.1 9.8 %custom-call.30 = f32[1,128,128]{1,2,0:T(8,128)S(1)} custom-call(f32[1,128,128]{2,1,0:T(8,128)S(1)} %get-tuple-element.62), custom_call_target="InvertDiagBlocksLowerTriangular" | custom-call | tf_op jit(solution)/shard_map/jit(cholesky)/cholesky | solution.py:126
  435.5 11.7 %cholesky.215 = f32[128,128]{1,0:T(8,128)S(1)} custom-call(f32[128,128]{1,0:T(8,128)S(1)} %cholesky.267), custom_call_target="Cholesky" | custom-call | tf_op jit(solution)/shard_map/jit(cholesky)/cholesky | solution.py:126
  448.6 10.0 %custom-call.31 = f32[1,128,128]{1,2,0:T(8,128)S(1)} custom-call(f32[1,128,128]{2,1,0:T(8,128)S(1)} %get-tuple-element.59), custom_call_target="InvertDiagBlocksLowerTriangular" | custom-call | tf_op jit(solution)/shard_map/jit(cholesky)/cholesky | solution.py:126
  460.1 11.7 %cholesky.236 = f32[128,128]{1,0:T(8,128)S(1)} custom-call(f32[128,128]{1,0:T(8,128)S(1)} %cholesky.272), custom_call_target="Cholesky" | custom-call | tf_op jit(solution)/shard_map/jit(cholesky)/cholesky | solution.py:126
  472.6 9.8 %custom-call.32 = f32[1,128,128]{1,2,0:T(8,128)S(1)} custom-call(f32[1,128,128]{2,1,0:T(8,128)S(1)} %get-tuple-element.56), custom_call_target="InvertDiagBlocksLowerTriangular" | custom-call | tf_op jit(solution)/shard_map/jit(cholesky)/cholesky | solution.py:126
  483.8 11.9 %cholesky.253 = f32[128,128]{1,0:T(8,128)S(1)} custom-call(f32[128,128]{1,0:T(8,128)S(1)} %convolution_subtract_fusion.6), custom_call_target="Cholesky" | custom-call | tf_op jit(solution)/shard_map/jit(cholesky)/cholesky | solution.py:126
  500.3 14.1 %while.2 = (s32[]{:T(128)}, f32[512,512]{1,0:T(8,128)}, s32[4,2]{0,1:T(2,128)S(1)}, f32[4,128,128]{2,1,0:T(8,128)}, s32[]{:T(128)}) while((s32[]{:T(128)}, f32[512,512]{1,0:T(8,128)}, s32[4,2]{0,1:T(2,128)S(1)}, f32[4,128,128]{2,1,0:T(8,128)}, s32[]{:T(128)}) %tuple.45), condition=%wide.while_cond.1, body=%wide.while_body.1.sunk | while | flops 2 | bytes 132705 | solution.py:127
  514.4 40.1 %custom-call.33 = f32[4,128,128]{1,2,0:T(8,128)S(1)} custom-call(f32[4,128,128]{2,1,0:T(8,128)} %get-tuple-element.24), custom_call_target="InvertDiagBlocksLowerTriangular" | custom-call | tf_op jit(solution)/shard_map/triangular_solve | solution.py:127
  571.7 120.7 %all-reduce.4.cloned.1.call-done = (f32[16,1,32,512]{3,2,1,0:T(8,128)}, f32[16,1,32,512]{3,2,1,0:T(8,128)}, f32[16,1,32,512]{3,2,1,0:T(8,128)}, f32[16,1,32,512]{3,2,1,0:T(8,128)}) async-done(((f32[16,1,32,512]{3,2,1,0:T(8,128)}, f32[16,1,32,512]{3,2,1,0:T(8,128)}, f32[16,1,32,512]{3,2,1,0:T(8,128)}, f32[16,1,32,512]{3,2,1,0:T(8,128)}), (f32[16,1,32,512]{3,2,1,0:T(8,128)}, f32[16,1,32,512]{3,2,1,0:T(8,128)}, ...) | async-done | bytes 4194320 | tf_op jit(solution)/shard_map/psum | solution.py:12
  695.8 6.8 convolution_subtract_fusion
  707.1 4.6 compare_select_fusion
  (211 shorter events, 109.3 us)
Async XLA Ops:
  25.0 8.6 %copy-start.7 = (s32[2,8192]{1,0:T(2,128)S(1)}, s32[2,8192]{1,0:T(2,128)}, u32[]{:S(2)}) copy-start(s32[2,8192]{1,0:T(2,128)} %param.7) | copy-start | bytes 196612
  25.0 178.4 %all-to-all-start = ((f32[512,8,128]{0,2,1:T(8,128)}), f32[512,8,128]{0,2,1:T(8,128)S(1)}, u32[]{:S(2)}, u32[]{:S(2)}) async-start(f32[512,8,128]{0,2,1:T(8,128)} %bitcast.218), calls=%async_computation | async-start | bytes 4194304 | tf_op jit(solution)/shard_map/all_to_all | solution.py:73
  203.3 1.3 copy-start.4
  214.0 53.0 %all-to-all-start.1 = ((f32[32,24,1024]{2,1,0:T(8,128)}), f32[32,24,1024]{2,1,0:T(8,128)}, u32[]{:S(2)}, u32[]{:S(2)}) async-start(f32[32,24,1024]{2,1,0:T(8,128)} %broadcast_select_fusion), calls=%async_computation.1 | async-start | bytes 6291456 | tf_op jit(solution)/shard_map/all_to_all | solution.py:75
  221.6 135.5 %all-gather.3.cloned.1.call-start = ((), (), s32[]{:S(2)}) async-start(), calls=%async_computation.2 | async-start | bytes 1179648 | tf_op jit(solution)/shard_map/all_gather | solution.py:114
  283.8 5.5 copy-start
  313.8 2.0 copy-start.1
  316.6 90.0 %all-gather.5.cloned.1.call-start = ((), (), s32[]{:S(2)}) async-start(), calls=%async_computation.3 | async-start | bytes 2162688 | tf_op jit(solution)/shard_map/all_gather | solution.py:121
  359.1 333.3 %all-reduce.4.cloned.1.call-start = ((), (), s32[]{:S(2)}) async-start(), calls=%async_computation.4 | async-start | bytes 8388608 | tf_op jit(solution)/shard_map/psum | solution.py:12
  410.2 1.0 copy-start.5
  500.3 61.2 %copy-start.6 = (f32[512,128]{1,0:T(8,128)S(1)}, f32[512,128]{1,0:T(8,128)}, u32[]{:S(2)}) copy-start(f32[512,128]{1,0:T(8,128)} %copy.90) | copy-start | bytes 786436
  554.5 0.7 copy-start.8
  692.4 3.4 copy-start.2
  702.7 2.0 copy-start.3
Sparse Core Ops, SparseCore 0:
  316.7 40.3 all-gather.2
  359.7 46.8 all-gather.4
  569.8 122.5 all-reduce.3
where the time goes:
time: 728 us; the launch traced here: 719 us
  other arithmetic  273 us (38%)
  waiting for transfers between devices  205 us (28%)
  local copies, waits for them, and re-layouts  185 us (25%)
  matrix products  22.3 us (3%)
  between operations  17.1 us (2%)
  starting transfers between devices  16.8 us (2%)
    psum x1, waiting for transfers between devices, from_root(): return lax.psum(kept, axis)  121 us
    scatter-add x2, other arithmetic, body(): taken = jnp.nonzero(col_mask, size=received_cols)[0]  114 us
    another operation x15, other arithmetic, body(): factor = jnp.linalg.cholesky(pivot)  79.5 us
    scatter x2, local copies, waits for them, and re-layouts, body(): row_index = jnp.full((slots_child,), local_rows, jnp.int32).at[slots].set...  61.1 us
    all_gather x1, waiting for transfers between devices, body(): lax.all_gather(panel[:head_blocks * NB], ('sub', 'row'), axis=0, tiled=True)  43.7 us
    another operation x3, other arithmetic, body(): lax.linalg.triangular_solve(factor, panel, left_side=False, lower=True, t...  41.4 us
    all_gather x1, waiting for transfers between devices, body(): lax.all_gather(assembled[:, :panel_local], 'col', axis=1, tiled=True)  40.4 us
    gather x8, local copies, waits for them, and re-layouts, body(): received[child][jnp.minimum(slot_of_row, slots_child - 1)]  37.8 us
  transfers between devices with their start and end apart: 5, of which 3 were waited for; matrix products, arithmetic and copies ran while one was open for 31% of the time, Pallas kernels for 0%

commit v1 on v0

--- a/solution.py
+++ b/solution.py
@@ -5,6 +5,12 @@
 
 PW = 512
 NB = 32
+
+
+def laid_out(pieces, dim):
+    shape = list(pieces.shape[1:])
+    shape[dim] *= pieces.shape[0]
+    return jnp.moveaxis(pieces, 0, dim).reshape(shape)
 
 
 def from_root(value, axis, source):
@@ -111,7 +117,20 @@
             row_inside[:, None] & col_inside[None, :], placed, jnp.float32(0.0)
         )
     panel_local = PW // n_col
-    gathered = lax.all_gather(assembled[:, :panel_local], "col", axis=1, tiled=True)
+    shard = assembled[:, :panel_local]
+    size = lax.axis_size("col")
+    pairs = [(i, (i + 1) % size) for i in range(size)]
+    back = [(b, a) for a, b in pairs]
+    lower_2, upper = ([], [])
+    for lap in range(size - 1):
+        if lap % 2 == 0:
+            lower_2.append(lax.ppermute(lower_2[-1] if lower_2 else shard, "col", pairs))
+        else:
+            upper.append(lax.ppermute(upper[-1] if upper else shard, "col", back))
+    blocks = jnp.stack([*lower_2[::-1], shard, *upper])
+    shift = lax.axis_index("col") - len(lower_2)
+    blocks = blocks[(jnp.arange(size) - shift) % size]
+    gathered = laid_out(blocks, 1)
     panel = (
         gathered.reshape(local_rows, n_col, panel_local // NB, NB)
         .transpose(0, 2, 1, 3)

time: 728 us -> 723 us (level)
  waiting for transfers between devices: 205 us -> 191 us
  starting transfers between devices: 16.8 us -> 28.4 us
  matrix products: 22.3 us -> 14.7 us
    all_gather x1 -> x0, waiting for transfers between devices: 40.4 us -> none  [body(): lax.all_gather(assembled[:, :panel_local], 'col', axis=1, tiled=True)]
    ppermute x0 -> x7, waiting for transfers between devices: none -> 23.2 us  [the longest x4 23.2 us: body(): lax.ppermute(lower_2[-1] if lower_2 else shard, 'col', pairs)]
    ppermute x0 -> x7, starting transfers between devices: none -> 11.9 us  [the longest x3 9.53 us: body(): upper.append(lax.ppermute(upper[-1] if upper else shard, 'col', back))]
    another operation x27 -> x28, local copies, waits for them, and re-layouts: 15.8 us -> 16.5 us
  transfers between devices with their start and end apart: 5 -> 11, of which waited for: 3 -> 6; matrix products, arithmetic and copies ran while one was open for 31% -> 31% of each run, Pallas kernels for 0% -> 0%
where the time goes in v1:
time: 723 us; the launch traced here: 715 us
  other arithmetic  273 us (38%)
  waiting for transfers between devices  191 us (26%)
  local copies, waits for them, and re-layouts  190 us (26%)
  starting transfers between devices  28.4 us (4%)
  between operations  17.2 us (2%)
  matrix products  14.7 us (2%)
    psum x1, waiting for transfers between devices, from_root(): return lax.psum(kept, axis)  121 us
    scatter-add x2, other arithmetic, body(): taken = jnp.nonzero(col_mask, size=received_cols)[0]  114 us
    another operation x15, other arithmetic, body(): factor = jnp.linalg.cholesky(pivot)  79.7 us
    scatter x2, local copies, waits for them, and re-layouts, body(): row_index = jnp.full((slots_child,), local_rows, jnp.int32).at[slots].set...  61.3 us
    all_gather x1, waiting for transfers between devices, body(): lax.all_gather(panel[:head_blocks * NB], ('sub', 'row'), axis=0, tiled=True)  47.5 us
    another operation x3, other arithmetic, body(): lax.linalg.triangular_solve(factor, panel, left_side=False, lower=True, t...  41.4 us
    gather x8, local copies, waits for them, and re-layouts, body(): received[child][jnp.minimum(slot_of_row, slots_child - 1)]  37.8 us
    ppermute x4, waiting for transfers between devices, body(): lax.ppermute(lower_2[-1] if lower_2 else shard, 'col', pairs)  23.2 us
  transfers between devices with their start and end apart: 11, of which 6 were waited for; matrix products, arithmetic and copies ran while one was open for 31% of the time, Pallas kernels for 0%

profile of v1, /device:TPU:6, one launch (start us, length us, event | category | flops | bytes accessed | tf_op | source)
XLA Modules:
  0.0 714.6 jit_solution(5475664692647860487)
XLA Ops:
  20.1 4.9 gather_fusion.1
  25.0 8.6 %all-to-all-start = ((f32[512,8,128]{0,2,1:T(8,128)}), f32[512,8,128]{0,2,1:T(8,128)S(1)}, u32[]{:S(2)}, u32[]{:S(2)}) async-start(f32[512,8,128]{0,2,1:T(8,128)} %bitcast.237), calls=%async_computation | async-start | bytes 4194304 | tf_op jit(solution)/shard_map/all_to_all | solution.py:79
  39.4 56.9 %scatter_custom_fusion.2 = s32[1024]{0:T(1024)S(1)} fusion(s32[8192]{0:T(1024)S(1)} %bitcast.260, s32[8192]{0:T(1024)S(1)} %ne.688, s32[]{:T(128)} %constant.522.clone.1), kind=kCustom, calls=%fused_computation.431 | custom fusion | flops 8192 | bytes 4100 | tf_op jit(solution)/shard_map/scatter-add | solution.py:88
  101.6 6.2 gather_fusion
  107.8 56.8 %scatter_custom_fusion.8 = s32[1024]{0:T(1024)S(1)} fusion(s32[8192]{0:T(1024)S(1)} %bitcast.259, s32[8192]{0:T(1024)S(1)} %ne.688, s32[]{:T(128)} %constant.522.clone.1), kind=kCustom, calls=%fused_computation.429 | custom fusion | flops 8192 | bytes 4100 | tf_op jit(solution)/shard_map/scatter-add | solution.py:88
  165.9 6.2 gather_fusion.5
  172.7 30.9 %scatter_custom_fusion = s32[384]{0:T(512)S(1)} fusion(s32[8192]{0:T(1024)S(1)} %bitcast.258, s32[8192]{0:T(1024)S(1)} %get-tuple-element.68, s32[]{:T(128)} %constant.534.clone.1), kind=kCustom, calls=%fused_computation.447 | custom fusion | bytes 1540 | tf_op jit(solution)/shard_map/scatter | solution.py:99
  214.3 7.6 %all-to-all-start.1 = ((f32[32,24,1024]{2,1,0:T(8,128)}), f32[32,24,1024]{2,1,0:T(8,128)}, u32[]{:S(2)}, u32[]{:S(2)}) async-start(f32[32,24,1024]{2,1,0:T(8,128)} %broadcast_select_fusion), calls=%async_computation.1 | async-start | bytes 6291456 | tf_op jit(solution)/shard_map/all_to_all | solution.py:81
  222.0 4.3 scatter_custom_fusion.3
  226.4 30.4 %scatter_custom_fusion.6 = s32[384]{0:T(512)S(1)} fusion(s32[8192]{0:T(1024)S(1)} %bitcast.257, s32[8192]{0:T(1024)S(1)} %get-tuple-element.65, s32[]{:T(128)} %constant.534.clone.1), kind=kCustom, calls=%fused_computation.445 | custom fusion | bytes 1540 | tf_op jit(solution)/shard_map/scatter | solution.py:99
  262.8 4.5 scatter_custom_fusion.9
  275.4 8.9 %gather_fusion.4 = f32[2048,512]{1,0:T(8,128)} fusion(f32[512,1024]{0,1:T(8,128)S(1)} %copy.27, s32[2048]{0:T(1024)S(1)} %fusion.85), kind=kCustom, calls=%fused_computation.4 | custom fusion | bytes 8396800 | tf_op jit(solution)/shard_map/gather | solution.py:113
  284.3 5.5 copy.28
  294.3 8.9 %gather_fusion.7 = f32[2048,512]{1,0:T(8,128)} fusion(f32[512,1024]{0,1:T(8,128)S(1)} %copy.34, s32[2048]{0:T(1024)S(1)} %fusion.86), kind=kCustom, calls=%fused_computation.7 | custom fusion | bytes 8396800 | tf_op jit(solution)/shard_map/gather | solution.py:113
  303.2 5.4 copy.35
  308.6 5.6 fusion.1
  318.4 8.1 %collective-permute-done = f32[512,64]{1,0:T(8,128)S(1)} collective-permute-done((f32[512,64]{1,0:T(8,128)S(1)}, f32[512,64]{1,0:T(8,128)S(1)}, u32[]{:S(2)}, u32[]{:S(2)}) %collective-permute-start) | collective-permute-done | bytes 131104 | tf_op jit(solution)/shard_map/ppermute | solution.py:127
  329.8 5.9 collective-permute-done.1
  338.9 5.0 collective-permute-done.2
  363.5 47.5 %all-gather.2.cloned.1.call-done = f32[1024,512]{1,0:T(8,128)} async-done(((f32[32,512]{1,0:T(8,128)}), f32[1024,512]{1,0:T(8,128)}) %all-gather.2.cloned.1.call-update) | async-done | bytes 2097168 | tf_op jit(solution)/shard_map/all_gather | solution.py:140
  414.6 11.7 %cholesky.103 = f32[128,128]{1,0:T(8,128)S(1)} custom-call(f32[128,128]{1,0:T(8,128)S(1)} %cholesky.263), custom_call_target="Cholesky" | custom-call | tf_op jit(solution)/shard_map/jit(cholesky)/cholesky | solution.py:145
  426.5 9.8 %custom-call.30 = f32[1,128,128]{1,2,0:T(8,128)S(1)} custom-call(f32[1,128,128]{2,1,0:T(8,128)S(1)} %get-tuple-element.59), custom_call_target="InvertDiagBlocksLowerTriangular" | custom-call | tf_op jit(solution)/shard_map/jit(cholesky)/cholesky | solution.py:145
  437.0 11.7 %cholesky.215 = f32[128,128]{1,0:T(8,128)S(1)} custom-call(f32[128,128]{1,0:T(8,128)S(1)} %cholesky.267), custom_call_target="Cholesky" | custom-call | tf_op jit(solution)/shard_map/jit(cholesky)/cholesky | solution.py:145
  450.1 10.2 %custom-call.31 = f32[1,128,128]{1,2,0:T(8,128)S(1)} custom-call(f32[1,128,128]{2,1,0:T(8,128)S(1)} %get-tuple-element.56), custom_call_target="InvertDiagBlocksLowerTriangular" | custom-call | tf_op jit(solution)/shard_map/jit(cholesky)/cholesky | solution.py:145
  460.9 11.7 %cholesky.236 = f32[128,128]{1,0:T(8,128)S(1)} custom-call(f32[128,128]{1,0:T(8,128)S(1)} %cholesky.272), custom_call_target="Cholesky" | custom-call | tf_op jit(solution)/shard_map/jit(cholesky)/cholesky | solution.py:145
  473.4 9.8 %custom-call.32 = f32[1,128,128]{1,2,0:T(8,128)S(1)} custom-call(f32[1,128,128]{2,1,0:T(8,128)S(1)} %get-tuple-element.53), custom_call_target="InvertDiagBlocksLowerTriangular" | custom-call | tf_op jit(solution)/shard_map/jit(cholesky)/cholesky | solution.py:145
  483.8 11.9 %cholesky.253 = f32[128,128]{1,0:T(8,128)S(1)} custom-call(f32[128,128]{1,0:T(8,128)S(1)} %convolution_subtract_fusion.6), custom_call_target="Cholesky" | custom-call | tf_op jit(solution)/shard_map/jit(cholesky)/cholesky | solution.py:145
  500.3 14.1 %while.2 = (s32[]{:T(128)}, f32[512,512]{1,0:T(8,128)}, s32[4,2]{0,1:T(2,128)S(1)}, f32[4,128,128]{2,1,0:T(8,128)}, s32[]{:T(128)}) while((s32[]{:T(128)}, f32[512,512]{1,0:T(8,128)}, s32[4,2]{0,1:T(2,128)S(1)}, f32[4,128,128]{2,1,0:T(8,128)}, s32[]{:T(128)}) %tuple.44), condition=%wide.while_cond.1, body=%wide.while_body.1.sunk | while | flops 2 | bytes 132705 | solution.py:146
  514.3 40.1 %custom-call.33 = f32[4,128,128]{1,2,0:T(8,128)S(1)} custom-call(f32[4,128,128]{2,1,0:T(8,128)} %get-tuple-element.24), custom_call_target="InvertDiagBlocksLowerTriangular" | custom-call | tf_op jit(solution)/shard_map/triangular_solve | solution.py:146
  567.5 120.8 %all-reduce.4.cloned.1.call-done = (f32[16,1,32,512]{3,2,1,0:T(8,128)}, f32[16,1,32,512]{3,2,1,0:T(8,128)}, f32[16,1,32,512]{3,2,1,0:T(8,128)}, f32[16,1,32,512]{3,2,1,0:T(8,128)}) async-done(((f32[16,1,32,512]{3,2,1,0:T(8,128)}, f32[16,1,32,512]{3,2,1,0:T(8,128)}, f32[16,1,32,512]{3,2,1,0:T(8,128)}, f32[16,1,32,512]{3,2,1,0:T(8,128)}), (f32[16,1,32,512]{3,2,1,0:T(8,128)}, f32[16,1,32,512]{3,2,1,0:T(8,128)}, ...) | async-done | bytes 4194320 | tf_op jit(solution)/shard_map/psum | solution.py:18
  691.7 6.8 convolution_subtract_fusion
  703.0 4.6 compare_select_fusion
  (224 shorter events, 130.4 us)
Async XLA Ops:
  25.0 8.6 %copy-start.6 = (s32[2,8192]{1,0:T(2,128)S(1)}, s32[2,8192]{1,0:T(2,128)}, u32[]{:S(2)}) copy-start(s32[2,8192]{1,0:T(2,128)} %param.7) | copy-start | bytes 196612
  25.0 178.6 %all-to-all-start = ((f32[512,8,128]{0,2,1:T(8,128)}), f32[512,8,128]{0,2,1:T(8,128)S(1)}, u32[]{:S(2)}, u32[]{:S(2)}) async-start(f32[512,8,128]{0,2,1:T(8,128)} %bitcast.237), calls=%async_computation | async-start | bytes 4194304 | tf_op jit(solution)/shard_map/all_to_all | solution.py:79
  203.6 1.3 copy-start.4
  214.3 53.1 %all-to-all-start.1 = ((f32[32,24,1024]{2,1,0:T(8,128)}), f32[32,24,1024]{2,1,0:T(8,128)}, u32[]{:S(2)}, u32[]{:S(2)}) async-start(f32[32,24,1024]{2,1,0:T(8,128)} %broadcast_select_fusion), calls=%async_computation.1 | async-start | bytes 6291456 | tf_op jit(solution)/shard_map/all_to_all | solution.py:81
  221.9 189.0 %all-gather.2.cloned.1.call-start = ((), (), s32[]{:S(2)}) async-start(), calls=%async_computation.2 | async-start | bytes 2162688 | tf_op jit(solution)/shard_map/all_gather | solution.py:140
  284.3 5.5 copy-start
  314.2 2.0 copy-start.1
  316.3 10.3 %collective-permute-start = (f32[512,64]{1,0:T(8,128)S(1)}, f32[512,64]{1,0:T(8,128)S(1)}, u32[]{:S(2)}, u32[]{:S(2)}) collective-permute-start(f32[512,64]{1,0:T(8,128)S(1)} %slice.282), channel_id=1, source_target_pairs={{0,1},{1,2},{2,3},{3,4},{4,5},{5,6},{6,7},{7,0},{8,9},{9,10},{10,1... | collective-permute-start | bytes 393224 | tf_op jit(solution)/shard_map/ppermute | solution.py:127
  326.6 9.1 %collective-permute-start.1 = (f32[512,64]{1,0:T(8,128)S(1)}, f32[512,64]{1,0:T(8,128)S(1)}, u32[]{:S(2)}, u32[]{:S(2)}) collective-permute-start(f32[512,64]{1,0:T(8,128)S(1)} %collective-permute-done), channel_id=1, source_target_pairs={{0,1},{1,2},{2,3},{3,4},{4,5},{5,6},{6,7},{7,0},{8,9},{9,10},{10,1... | collective-permute-start | bytes 393224 | tf_op jit(solution)/shard_map/ppermute | solution.py:127
  326.8 8.9 %collective-permute-start.4 = (f32[512,64]{1,0:T(8,128)S(1)}, f32[512,64]{1,0:T(8,128)S(1)}, u32[]{:S(2)}, u32[]{:S(2)}) collective-permute-start(f32[512,64]{1,0:T(8,128)S(1)} %slice.282), channel_id=1, source_target_pairs={{1,0},{2,1},{3,2},{4,3},{5,4},{6,5},{7,6},{0,7},{9,8},{10,9},{11,1... | collective-permute-start | bytes 393224 | tf_op jit(solution)/shard_map/ppermute | solution.py:129
  335.7 8.2 %collective-permute-start.2 = (f32[512,64]{1,0:T(8,128)S(1)}, f32[512,64]{1,0:T(8,128)S(1)}, u32[]{:S(2)}, u32[]{:S(2)}) collective-permute-start(f32[512,64]{1,0:T(8,128)S(1)} %collective-permute-done.1), channel_id=1, source_target_pairs={{0,1},{1,2},{2,3},{3,4},{4,5},{5,6},{6,7},{7,0},{8,9},{9,10},{10,1... | collective-permute-start | bytes 393224 | tf_op jit(solution)/shard_map/ppermute | solution.py:127
  335.7 8.2 %collective-permute-start.5 = (f32[512,64]{1,0:T(8,128)S(1)}, f32[512,64]{1,0:T(8,128)S(1)}, u32[]{:S(2)}, u32[]{:S(2)}) collective-permute-start(f32[512,64]{1,0:T(8,128)S(1)} %collective-permute-done.4), channel_id=1, source_target_pairs={{1,0},{2,1},{3,2},{4,3},{5,4},{6,5},{7,6},{0,7},{9,8},{10,9},{11,1... | collective-permute-start | bytes 393224 | tf_op jit(solution)/shard_map/ppermute | solution.py:129
  343.9 7.6 %collective-permute-start.3 = (f32[512,64]{1,0:T(8,128)S(1)}, f32[512,64]{1,0:T(8,128)S(1)}, u32[]{:S(2)}, u32[]{:S(2)}) collective-permute-start(f32[512,64]{1,0:T(8,128)S(1)} %collective-permute-done.2), channel_id=1, source_target_pairs={{0,1},{1,2},{2,3},{3,4},{4,5},{5,6},{6,7},{7,0},{8,9},{9,10},{10,1... | collective-permute-start | bytes 393224 | tf_op jit(solution)/shard_map/ppermute | solution.py:127
  343.9 13.6 %collective-permute-start.6 = (f32[512,64]{1,0:T(8,128)S(1)}, f32[512,64]{1,0:T(8,128)S(1)}, u32[]{:S(2)}, u32[]{:S(2)}) collective-permute-start(f32[512,64]{1,0:T(8,128)S(1)} %collective-permute-done.5), channel_id=1, source_target_pairs={{1,0},{2,1},{3,2},{4,3},{5,4},{6,5},{7,6},{0,7},{9,8},{10,9},{11,1... | collective-permute-start | bytes 393224 | tf_op jit(solution)/shard_map/ppermute | solution.py:129
  362.1 326.2 %all-reduce.4.cloned.1.call-start = ((), (), s32[]{:S(2)}) async-start(), calls=%async_computation.3 | async-start | bytes 8388608 | tf_op jit(solution)/shard_map/psum | solution.py:18
  483.8 70.7 %copy-start.5 = (f32[512,2,8,32]{0,3,2,1:T(8,128)S(1)}, f32[512,2,8,32]{0,3,2,1:T(8,128)}, u32[]{:S(2)}) copy-start(f32[512,2,8,32]{0,3,2,1:T(8,128)} %copy.40) | copy-start | bytes 3145732
  688.3 3.4 copy-start.2
  698.6 2.0 copy-start.3
Sparse Core Ops, SparseCore 0:
  362.2 48.7 all-gather.1
  565.6 122.5 all-reduce.3
